TPU v7x, 32 devices: a whole 2x2x4 slice. The times are simulated.
32 devices in a mesh: seq: 4 (over z), row: 8 (over y, x, core).
Axes of the slice: x: 2, y: 2, z: 4, core: 2. Of those that a mesh axis runs over, the one named last changes fastest.
Arguments:
- queries: bfloat16 [3, 128, 8192], P(None, 'row'), may hold values from -128 to 128
- prefix_keys: bfloat16 [6144, 512], P('seq'), may hold values from -6 to 6
- prefix_values: bfloat16 [6144, 512], P('seq'), may hold values from -6 to 6
- suffix_keys: bfloat16 [128, 256, 512], P('row', 'seq'), may hold values from -6 to 6
- suffix_values: bfloat16 [128, 256, 512], P('row', 'seq'), may hold values from -6 to 6
- new_keys: bfloat16 [3, 128, 512], P(None, 'row'), may hold values from -6 to 6
- new_values: bfloat16 [3, 128, 512], P(None, 'row'), may hold values from -6 to 6
- lengths: int32 [128], P('row'), may hold values from 16 to 256
- pair_of: int32 [128], replicated, may hold values from 0 to 127, as said below
- guidance: float32 [64], replicated, may hold values from 1 to 3
Outputs:
- guided: bfloat16 [3, 128, 8192], P(None, 'row', 'seq')
Inputs may be any that keep to these rules, and one draw needn't show every extreme that they name: pair_of[pair_of[r]] = r; a row of the first half of the 128 rows is paired with a row of the second half, and pair_of[r] // 16 = (r // 16 + 128 / 32) mod (8).
All inputs are finite; a program needn't handle non-finite values.
Results may differ from a plain program's by a relative error of at most 0.014.
Values may be sent and summed in bfloat16 or wider, within the bound.
No kernel may reach another device: no remote copies, remote signals or barrier semaphores. Data moves between devices by JAX's collectives and lax.ppermute only.
A program may use at most 128 MiB of HBM per device.

v0:
```python
import jax
import jax.numpy as jnp
from jax import lax
from jax.sharding import PartitionSpec as P

HD = 128


def shifted(value, axis, steps):
    count = lax.axis_size(axis)
    pairs = [(source, (source + steps) % count) for source in range(count)]
    return lax.ppermute(value, axis, pairs)


def local(
    queries,
    prefix_keys,
    prefix_values,
    suffix_keys,
    suffix_values,
    new_keys,
    new_values,
    lengths,
    pair_of,
    guidance,
):
    steps, row_dev, width = queries.shape
    kv_heads = prefix_keys.shape[1] // HD
    heads = width // HD
    group = heads // kv_heads
    scale = HD ** (-0.5)
    query = queries.reshape(steps, row_dev, kv_heads, group, HD)
    pre_keys = prefix_keys.reshape(-1, kv_heads, HD)
    pre_values = prefix_values.reshape(-1, kv_heads, HD)
    suf_keys = suffix_keys.reshape(row_dev, -1, kv_heads, HD)
    suf_values = suffix_values.reshape(row_dev, -1, kv_heads, HD)
    suf_dev = suf_keys.shape[1]
    pre_scores = (
        jnp.einsum("trkgd,nkd->trkgn", query, pre_keys, preferred_element_type=jnp.float32) * scale
    )
    suf_scores = (
        jnp.einsum("trkgd,rnkd->trkgn", query, suf_keys, preferred_element_type=jnp.float32) * scale
    )
    position = lax.axis_index("seq") * suf_dev + jnp.arange(suf_dev, dtype=jnp.int32)
    live = position[None, :] < lengths[:, None]
    suf_scores = jnp.where(live[None, :, None, None, :], suf_scores, -1e30)
    top = jnp.maximum(jnp.max(pre_scores, -1), jnp.max(suf_scores, -1))
    pre_weights = jnp.exp(pre_scores - top[..., None])
    suf_weights = jnp.exp(suf_scores - top[..., None])
    total = jnp.sum(pre_weights, -1) + jnp.sum(suf_weights, -1)
    summed = jnp.einsum(
        "trkgn,nkd->trkgd",
        pre_weights.astype(jnp.bfloat16),
        pre_values,
        preferred_element_type=jnp.float32,
    )
    summed = summed + jnp.einsum(
        "trkgn,rnkd->trkgd",
        suf_weights.astype(jnp.bfloat16),
        suf_values,
        preferred_element_type=jnp.float32,
    )
    top = top.reshape(steps, row_dev, heads)
    total = total.reshape(steps, row_dev, heads)
    summed = summed.reshape(steps, row_dev, heads, HD)
    shards = lax.axis_size("seq")
    share = heads // shards
    first = lax.axis_index("seq") * share
    pieces = (
        lax.all_to_all(top[None], "seq", split_axis=3, concat_axis=0, tiled=True),
        lax.all_to_all(total[None], "seq", split_axis=3, concat_axis=0, tiled=True),
        lax.all_to_all(summed[None], "seq", split_axis=3, concat_axis=0, tiled=True),
    )
    top_own = jnp.max(pieces[0], 0)
    factor = jnp.exp(pieces[0] - top_own[None])
    total_own = jnp.sum(pieces[1] * factor, 0)
    summed_own = jnp.sum(pieces[2] * factor[..., None], 0)
    fresh_keys = new_keys.reshape(steps, row_dev, kv_heads, HD)
    fresh_values = new_values.reshape(steps, row_dev, kv_heads, HD)
    step_index = jnp.arange(steps, dtype=jnp.int32)
    causal = step_index[None, :] <= step_index[:, None]
    new_scores = (
        jnp.einsum("trkgd,jrkd->trkgj", query, fresh_keys, preferred_element_type=jnp.float32)
        * scale
    )
    new_scores = jnp.where(causal[:, None, None, None, :], new_scores, -1e30)
    new_scores = lax.dynamic_slice_in_dim(
        new_scores.reshape(steps, row_dev, heads, steps), first, share, 2
    )
    kv_index = (first + jnp.arange(share, dtype=jnp.int32)) // group
    own_values = jnp.take(fresh_values, kv_index, axis=2)
    highest = jnp.maximum(top_own, jnp.max(new_scores, -1))
    new_weights = jnp.exp(new_scores - highest[..., None])
    factor = jnp.exp(top_own - highest)
    total_own = total_own * factor + jnp.sum(new_weights, -1)
    summed_own = summed_own * factor[..., None] + jnp.einsum(
        "trhj,jrhd->trhd",
        new_weights.astype(jnp.bfloat16),
        own_values,
        preferred_element_type=jnp.float32,
    )
    attention = (summed_own / total_own[..., None]).astype(jnp.bfloat16)
    mine = lax.axis_index("row") * row_dev + jnp.arange(row_dev, dtype=jnp.int32)
    partner = jnp.take(pair_of, mine)
    across = shifted(attention, "row", lax.axis_size("row") // 2)
    other = jnp.take(across, partner % row_dev, axis=1)
    lower = (mine < partner)[None, :, None, None]
    cond = jnp.where(lower, attention, other).astype(jnp.float32)
    uncond = jnp.where(lower, other, attention).astype(jnp.float32)
    scales = lax.dynamic_slice_in_dim(guidance, first, share, 0)
    mix = uncond + scales[None, None, :, None] * (cond - uncond)
    norm = jnp.sqrt(jnp.mean(mix * mix, -1, keepdims=True) + 1e-06)
    return (mix / norm).reshape(steps, row_dev, share * HD).astype(jnp.bfloat16)


def solution(mesh):
    placed = (
        P(None, "row", None),
        P("seq", None),
        P("seq", None),
        P("row", "seq", None),
        P("row", "seq", None),
        P(None, "row", None),
        P(None, "row", None),
        P("row"),
        P(),
        P(),
    )
    return jax.shard_map(
        local, mesh=mesh, in_specs=placed, out_specs=P(None, "row", "seq"), check_vma=False
    )
```

profile of v0, /device:TPU:0, one launch (start us, length us, event | category | flops | bytes accessed | tf_op | source)
XLA Modules:
  0.0 110.3 jit_solution(17701775485148774721)
XLA Ops:
  0.0 1.4 %copy.227 = bf16[6,8,64,128]{3,2,1,0:T(8,128)(2,1)S(1)} copy(bf16[6,8,64,128]{3,1,2,0:T(8,128)(2,1)} %bitcast.118) | data formatting | bytes 1572864
  1.8 2.4 %reshape.311 = bf16[1536,4,128]{2,1,0:T(4,128)(2,1)S(1)} reshape(bf16[1536,512]{1,0:T(8,128)(2,1)} %param.11) | data formatting | bytes 3145728 | tf_op jit(solution)/shard_map/reshape | solution.py:33
  4.2 7.9 %bitcast_reduce_fusion = (f32[3,16,4,16]{3,1,0,2:T(8,128)S(1)}, f32[4,1536,3,16,16]{1,4,3,2,0:T(8,128)}) fusion(bf16[3,16,4,16,128]{4,3,2,1,0:T(8,128)(2,1)S(1)} %bitcast.113, bf16[1536,4,128,1,1]{2,1,0,4,3:T(4,128)(2,1)S(1)} %bitcast.110), kind=kOutput, calls=%fused_computation.4 | convolution fusion | flops 1217393664 | bytes 21245952 | tf_op jit(solution)/shard_map/trkgd,nkd->trkgn/dot_general | solution.py:39
  12.1 1.9 %bitcast_reduce_fusion.1 = (f32[3,16,4,16]{3,0,2,1:T(4,128)S(1)}, f32[16,4,64,3,16]{2,4,3,1,0:T(8,128)}) fusion(bf16[3,16,4,16,128]{4,3,2,1,0:T(8,128)(2,1)S(1)} %bitcast.114, bf16[16,64,4,128,1]{3,2,1,0,4:T(4,128)(2,1)S(1)} %bitcast.117, pred[16,64]{1,0:T(8,128)(4,1)S(1)} %broadcast_compare_fusion), kind=kOutput, calls=%fused_computation.16 | convolution fusion | flops 50918400 | bytes 2634752 | tf_op jit(solution)/shard_map/trkgd,rnkd->trkgn/dot_general | solution.py:42
  14.1 9.7 %fusion.1 = f32[3,16,4,16]{3,1,0,2:T(8,128)S(1)} fusion(f32[4,1536,3,16,16]{1,4,3,2,0:T(8,128)} %get-tuple-element.16, f32[3,16,4,16]{3,1,0,2:T(8,128)S(1)} %copy_maximum_fusion), kind=kLoop, calls=%fused_computation.6 | loop fusion | flops 14152704 | bytes 18898944 | tf_op jit(solution)/shard_map/reduce_sum | solution.py:50
  23.9 1.4 %fusion.12 = (f32[3,16,4,16]{3,0,2,1:T(4,128)S(1)}, bf16[3,16,4,16,64]{4,3,0,2,1:T(8,128)(2,1)}) fusion(f32[16,4,64,3,16]{2,4,3,1,0:T(8,128)S(1)} %copy-done.6, f32[3,16,4,16]{3,0,2,1:T(4,128)S(1)} %copy.186), kind=kLoop, calls=%fused_computation.21 | loop fusion | flops 586752 | bytes 1204224 | tf_op jit(solution)/shard_map/reduce_sum | solution.py:50
  25.6 0.6 broadcast.378
  26.2 0.9 reduce.3
  27.1 0.7 reshape.352
  27.9 6.3 %all-to-all-start.2 = ((f32[4,1,768]{2,1,0:T(1,128)}), f32[4,1,768]{2,1,0:T(1,128)S(1)}, u32[]{:S(2)}, u32[]{:S(2)}) async-start(f32[4,1,768]{2,1,0:T(1,128)} %reshape.352), calls=%async_computation.2 | async-start | bytes 24576 | tf_op jit(solution)/shard_map/all_to_all | solution.py:71
  34.2 0.8 reshape.316
  35.5 8.0 %fusion.3 = f32[4,3,16,16,128]{4,3,2,1,0:T(8,128)S(1)} fusion(f32[4,1536,3,16,16]{1,4,3,2,0:T(8,128)} %get-tuple-element.16, f32[3,16,4,16]{3,1,0,2:T(8,128)S(1)} %copy_maximum_fusion, bf16[1536,4,128,1,1]{2,1,0,4,3:T(4,128)(2,1)S(1)} %bitcast.112), kind=kOutput, calls=%fused_computation.8 | convolution fusion | flops 1222115328 | bytes 22032384 | tf_op jit(solution)/shard_map/trkgn,nkd->trkgd/dot_general | solution.py:51
  43.5 2.2 %reshape.315 = bf16[16,64,4,128]{3,2,1,0:T(4,128)(2,1)} reshape(bf16[16,64,512]{2,1,0:T(8,128)(2,1)} %param.14) | data formatting | bytes 2097152 | tf_op jit(solution)/shard_map/reshape | solution.py:36
  45.8 2.2 %fusion.15 = f32[3,16,4,16,3]{3,4,0,2,1:T(4,128)} fusion(bf16[3,16,4,16,128]{4,3,2,1,0:T(8,128)(2,1)S(1)} %bitcast.115, pred[3,3]{1,0:T(4,128)(4,1)S(1)} %iota_compare_fusion, bf16[3,16,4,128,1]{3,2,1,0,4:T(4,128)(2,1)S(1)} %bitcast.123), kind=kOutput, calls=%fused_computation.25 | convolution fusion | flops 2377728 | bytes 872457 | tf_op jit(solution)/shard_map/trkgd,jrkd->trkgj/dot_general | solution.py:83
  48.0 1.7 %bitcast_add_fusion = f32[3,16,4,16,128]{4,3,1,0,2:T(8,128)S(1)} fusion(f32[4,3,16,16,128]{4,3,2,1,0:T(8,128)S(1)} %fusion.3, bf16[16,64,4,128,1]{3,2,1,0,4:T(4,128)(2,1)S(1)} %bitcast.116, bf16[3,16,4,16,64]{4,3,0,2,1:T(8,128)(2,1)} %get-tuple-element.12), kind=kOutput, calls=%fused_computation.13 | convolution fusion | flops 50724864 | bytes 4587520 | tf_op jit(solution)/shard_map/trkgn,rnkd->trkgd/dot_general | solution.py:57
  50.0 0.9 reduce.1
  50.9 0.7 reshape.350
  51.7 5.1 %all-to-all-start.1 = ((f32[4,1,768]{2,1,0:T(1,128)}), f32[4,1,768]{2,1,0:T(1,128)S(1)}, u32[]{:S(2)}, u32[]{:S(2)}) async-start(f32[4,1,768]{2,1,0:T(1,128)} %reshape.350), calls=%async_computation.1 | async-start | bytes 24576 | tf_op jit(solution)/shard_map/all_to_all | solution.py:70
  56.8 1.1 copy.197
  58.3 2.1 %copy.190 = f32[1,3,16,64,128]{4,2,1,0,3:T(8,128)} copy(f32[1,3,16,64,128]{4,3,2,1,0:T(8,128)S(1)} %bitcast.111) | data formatting | bytes 3145728 | tf_op jit(solution)/shard_map/broadcast_in_dim;reshape | solution.py:72
  60.3 2.0 %all-to-all-done.1 = f32[4,1,768]{2,1,0:T(1,128)S(1)} async-done(((f32[4,1,768]{2,1,0:T(1,128)}), f32[4,1,768]{2,1,0:T(1,128)S(1)}, u32[]{:S(2)}, u32[]{:S(2)}) %all-to-all-start.1) | async-done | bytes 12320 | tf_op jit(solution)/shard_map/all_to_all | solution.py:70
  62.4 3.6 %all-to-all-start = ((f32[1,3,16,64,128]{4,2,1,0,3:T(8,128)}), f32[1,3,16,64,128]{4,2,1,0,3:T(8,128)S(1)}, u32[]{:S(2)}, u32[]{:S(2)}) async-start(f32[1,3,16,64,128]{4,2,1,0,3:T(8,128)} %copy.190), calls=%async_computation | async-start | bytes 3145728 | tf_op jit(solution)/shard_map/all_to_all | solution.py:72
  66.0 0.6 gather_fusion.1
  66.6 0.7 gather_fusion
  67.6 0.7 reduce.4
  68.7 0.7 reduce.2
  71.0 30.4 %all-to-all-done = f32[1,3,16,64,128]{4,2,1,0,3:T(8,128)S(1)} async-done(((f32[1,3,16,64,128]{4,2,1,0,3:T(8,128)}), f32[1,3,16,64,128]{4,2,1,0,3:T(8,128)S(1)}, u32[]{:S(2)}, u32[]{:S(2)}) %all-to-all-start) | async-done | bytes 1572896 | tf_op jit(solution)/shard_map/all_to_all | solution.py:72
  101.4 0.6 fusion.7
  102.3 1.6 %collective-permute-start = (bf16[3,16,16,128]{3,2,1,0:T(8,128)(2,1)S(1)}, bf16[3,16,16,128]{3,2,1,0:T(8,128)(2,1)S(1)}, u32[]{:S(2)}, u32[]{:S(2)}) collective-permute-start(bf16[3,16,16,128]{3,2,1,0:T(8,128)(2,1)S(1)} %fusion.24), channel_id=1, source_target_pairs={{0,4},{1,5},{2,6},{3,7},{4,0},{5,1},{6,2},{7,3},{8,12},{9,13},{10,... | collective-permute-start | bytes 589832 | tf_op jit(solution)/shard_map/ppermute | solution.py:12
  103.9 4.4 %collective-permute-done = bf16[3,16,16,128]{3,2,1,0:T(8,128)(2,1)S(1)} collective-permute-done((bf16[3,16,16,128]{3,2,1,0:T(8,128)(2,1)S(1)}, bf16[3,16,16,128]{3,2,1,0:T(8,128)(2,1)S(1)}, u32[]{:S(2)}, u32[]{:S(2)}) %collective-permute-start) | collective-permute-done | bytes 196640 | tf_op jit(solution)/shard_map/ppermute | solution.py:12
  108.3 0.6 gather_fusion.2
  109.5 0.8 convert_element_type.31
  (65 shorter events, 4.9 us)
Async XLA Ops:
  0.0 65.9 %copy-start = (bf16[3,16,512]{2,1,0:T(8,128)(2,1)S(1)}, bf16[3,16,512]{2,1,0:T(8,128)(2,1)}, u32[]{:S(2)}) copy-start(bf16[3,16,512]{2,1,0:T(8,128)(2,1)} %param.16) | copy-start | bytes 147460
  0.0 1.5 %copy-start.7 = (bf16[16,64,512]{2,1,0:T(8,128)(2,1)S(1)}, bf16[16,64,512]{2,1,0:T(8,128)(2,1)}, u32[]{:S(2)}) copy-start(bf16[16,64,512]{2,1,0:T(8,128)(2,1)} %param.13) | copy-start | bytes 3145732
  1.4 10.7 %copy-start.2 = (bf16[6,8,64,128]{3,2,1,0:T(8,128)(2,1)}, bf16[6,8,64,128]{3,2,1,0:T(8,128)(2,1)S(1)}, u32[]{:S(2)}) copy-start(bf16[6,8,64,128]{3,2,1,0:T(8,128)(2,1)S(1)} %copy.227) | copy-start | bytes 2359300
  1.8 2.4 %copy-start.8 = (s32[16]{0:T(128)S(1)}, s32[16]{0:T(128)}, u32[]{:S(2)}) copy-start(s32[16]{0:T(128)} %param.17) | copy-start | bytes 196
  14.1 9.8 %copy-start.6 = (f32[16,4,64,3,16]{2,4,3,1,0:T(8,128)S(1)}, f32[16,4,64,3,16]{2,4,3,1,0:T(8,128)}, u32[]{:S(2)}) copy-start(f32[16,4,64,3,16]{2,4,3,1,0:T(8,128)} %get-tuple-element.18) | copy-start | bytes 2359300
  23.9 11.2 %copy-start.5 = (bf16[1536,512]{1,0:T(8,128)(2,1)S(1)}, bf16[1536,512]{1,0:T(8,128)(2,1)}, u32[]{:S(2)}) copy-start(bf16[1536,512]{1,0:T(8,128)(2,1)} %param.12) | copy-start | bytes 4718596
  27.9 23.8 %all-to-all-start.2 = ((f32[4,1,768]{2,1,0:T(1,128)}), f32[4,1,768]{2,1,0:T(1,128)S(1)}, u32[]{:S(2)}, u32[]{:S(2)}) async-start(f32[4,1,768]{2,1,0:T(1,128)} %reshape.352), calls=%async_computation.2 | async-start | bytes 24576 | tf_op jit(solution)/shard_map/all_to_all | solution.py:71
  43.5 2.2 %copy-start.3 = (bf16[6,8,64,128]{3,2,1,0:T(8,128)(2,1)S(1)}, bf16[6,8,64,128]{3,2,1,0:T(8,128)(2,1)}, u32[]{:S(2)}) copy-start(bf16[6,8,64,128]{3,2,1,0:T(8,128)(2,1)} %copy-done.2) | copy-start | bytes 2359300
  45.8 2.2 %copy-start.4 = (bf16[16,64,4,128]{3,2,1,0:T(4,128)(2,1)S(1)}, bf16[16,64,4,128]{3,2,1,0:T(4,128)(2,1)}, u32[]{:S(2)}) copy-start(bf16[16,64,4,128]{3,2,1,0:T(4,128)(2,1)} %reshape.315) | copy-start | bytes 3145732
  51.7 10.7 %all-to-all-start.1 = ((f32[4,1,768]{2,1,0:T(1,128)}), f32[4,1,768]{2,1,0:T(1,128)S(1)}, u32[]{:S(2)}, u32[]{:S(2)}) async-start(f32[4,1,768]{2,1,0:T(1,128)} %reshape.350), calls=%async_computation.1 | async-start | bytes 24576 | tf_op jit(solution)/shard_map/all_to_all | solution.py:70
  60.3 6.3 %copy-start.1 = (s32[128]{0:T(128)S(1)}, s32[128]{0:T(128)}, u32[]{:S(2)}) copy-start(s32[128]{0:T(128)} %param.18) | copy-start | bytes 1540
  60.3 6.9 %copy-start.9 = (f32[64]{0:T(128)S(1)}, f32[64]{0:T(128)}, u32[]{:S(2)}) copy-start(f32[64]{0:T(128)} %param.19) | copy-start | bytes 772
  62.4 39.0 %all-to-all-start = ((f32[1,3,16,64,128]{4,2,1,0,3:T(8,128)}), f32[1,3,16,64,128]{4,2,1,0,3:T(8,128)S(1)}, u32[]{:S(2)}, u32[]{:S(2)}) async-start(f32[1,3,16,64,128]{4,2,1,0,3:T(8,128)} %copy.190), calls=%async_computation | async-start | bytes 3145728 | tf_op jit(solution)/shard_map/all_to_all | solution.py:72
  102.3 6.0 %collective-permute-start = (bf16[3,16,16,128]{3,2,1,0:T(8,128)(2,1)S(1)}, bf16[3,16,16,128]{3,2,1,0:T(8,128)(2,1)S(1)}, u32[]{:S(2)}, u32[]{:S(2)}) collective-permute-start(bf16[3,16,16,128]{3,2,1,0:T(8,128)(2,1)S(1)} %fusion.24), channel_id=1, source_target_pairs={{0,4},{1,5},{2,6},{3,7},{4,0},{5,1},{6,2},{7,3},{8,12},{9,13},{10,... | collective-permute-start | bytes 589832 | tf_op jit(solution)/shard_map/ppermute | solution.py:12
where the time goes:
time: 111 us; the launch traced here: 110 us
  waiting for transfers between devices  36.8 us (33%)
  matrix products  22.2 us (20%)
  local copies, waits for them, and re-layouts  17.6 us (16%)
  other arithmetic  16.7 us (15%)
  starting transfers between devices  16.6 us (15%)
    all_to_all x1, waiting for transfers between devices, local(): lax.all_to_all(summed[None], 'seq', split_axis=3, concat_axis=0, tiled=True)  30.4 us
    reduce_sum x2, other arithmetic, local(): total = jnp.sum(pre_weights, -1) + jnp.sum(suf_weights, -1)  11.2 us
    dot_general x1, matrix products, local(): jnp.einsum('trkgn,nkd->trkgd', pre_weights.astype(jnp.bfloat16), pre_valu...  8.05 us
    dot_general x1, matrix products, local(): jnp.einsum('trkgd,nkd->trkgn', query, pre_keys, preferred_element_type=jn...  7.9 us
    all_to_all x1, starting transfers between devices, local(): lax.all_to_all(total[None], 'seq', split_axis=3, concat_axis=0, tiled=True)  6.34 us
    all_to_all x1, starting transfers between devices, local(): lax.all_to_all(top[None], 'seq', split_axis=3, concat_axis=0, tiled=True)  5.08 us
    ppermute x1, waiting for transfers between devices, shifted(): return lax.ppermute(value, axis, pairs)  4.39 us
    unnamed x26, local copies, waits for them, and re-layouts  3.91 us
  transfers between devices with their start and end apart: 4, of which 3 were waited for; matrix products, arithmetic and copies ran while one was open for 23% of the time, Pallas kernels for 0%

commit v1 on v0

v1 whole, which is shorter than its diff:
```python
import functools

import jax
import jax.numpy as jnp
from jax import lax
from jax.experimental import pallas as pl
from jax.experimental.pallas import tpu as pltpu
from jax.sharding import PartitionSpec as P

HD = 128
LOG2E = 1.4426950408889634
NEG = -1e30


def dot_nt(a, b):
    return lax.dot_general(a, b, (((1,), (1,)), ((), ())), preferred_element_type=jnp.float32)


def dot_nn(a, b):
    return lax.dot_general(a, b, (((1,), (0,)), ((), ())), preferred_element_type=jnp.float32)


def cdiv(a, b):
    return -(-a // b)


def lanes(x):
    return jnp.broadcast_to(x, (x.shape[0], HD))


def exp_weights(scores, top, scale):
    return jnp.exp2((scores - top) * scale)


def with_ones(values):
    return jnp.concatenate([values, jnp.ones_like(values)], axis=1)


def partial_kernel(
    own, chunk_rows, meta, lengths, q_ref, k_ref, v_ref, sk_ref, sv_ref, *rest
):
    if own:
        nk_ref, nv_ref, o_ref, lse_ref, qs, lses = rest
    else:
        o_ref, qs, lses = rest
    steps, row_dev, width = q_ref.shape
    share = width // HD
    per_row = steps * share
    rows = row_dev * per_row
    suf_dev = sk_ref.shape[1]
    scale = HD ** (-0.5) * LOG2E
    for t in range(steps):
        for g in range(share):
            qs[pl.ds(t * share + g, row_dev, stride=per_row), :] = q_ref[
                t, :, g * HD : (g + 1) * HD
            ].astype(jnp.float32)
    keys = k_ref[...]
    values = with_ones(v_ref[...])
    base = meta[2]
    if own:
        fresh = steps * row_dev
        new_keys = nk_ref[...].reshape(fresh, HD)
        new_values = with_ones(nv_ref[...].reshape(fresh, HD))
    for c in range(row_dev // chunk_rows):
        size = chunk_rows * per_row
        q = qs[c * size : (c + 1) * size, :].astype(jnp.bfloat16)
        pre = dot_nt(q, keys)
        top_pre = jnp.max(pre, axis=1, keepdims=True)
        sufs = []
        tops = []
        for p in range(chunk_rows // 2):
            r = c * chunk_rows + 2 * p
            sk = sk_ref[r : r + 2].reshape(2 * suf_dev, HD)
            s = dot_nt(q[p * 2 * per_row : (p + 1) * 2 * per_row], sk)
            lane = lax.broadcasted_iota(jnp.int32, s.shape, 1)
            second = lax.broadcasted_iota(jnp.int32, s.shape, 0) >= per_row
            live0 = jnp.clip(lengths[r] - base, 0, suf_dev)
            live1 = jnp.clip(lengths[r + 1] - base, 0, suf_dev)
            low = jnp.where(second, suf_dev, 0)
            high = jnp.where(second, suf_dev + live1, live0)
            s = jnp.where((lane >= low) & (lane < high), s, NEG)
            sufs.append(s)
            tops.append(jnp.max(s, axis=1, keepdims=True))
        top = jnp.maximum(top_pre, jnp.concatenate(tops, axis=0))
        if own:
            s = dot_nt(q, new_keys)
            row = lax.broadcasted_iota(jnp.int32, s.shape, 0)
            col = lax.broadcasted_iota(jnp.int32, s.shape, 1)
            same = (col % row_dev) == (c * chunk_rows + row // per_row)
            causal = (col // row_dev) <= ((row % per_row) // share)
            new = jnp.where(same & causal, s, NEG)
            top = jnp.maximum(top, jnp.max(new, axis=1, keepdims=True))
        w = exp_weights(pre, top, scale).astype(jnp.bfloat16)
        acc = dot_nn(w, values)
        parts = []
        for p in range(chunk_rows // 2):
            r = c * chunk_rows + 2 * p
            sv = with_ones(sv_ref[r : r + 2].reshape(2 * suf_dev, HD))
            part = slice(p * 2 * per_row, (p + 1) * 2 * per_row)
            w = exp_weights(sufs[p], top[part], scale).astype(jnp.bfloat16)
            parts.append(dot_nn(w, sv))
        acc = acc + jnp.concatenate(parts, axis=0)
        if own:
            w = exp_weights(new, top, scale).astype(jnp.bfloat16)
            acc = acc + dot_nn(w, new_values)
        total = acc[:, HD:]
        out = acc[:, :HD] / total
        lse = lanes(top * scale) + jnp.log2(total)
        o_ref[c * size : (c + 1) * size, :] = out.astype(o_ref.dtype)
        if own:
            lse_ref[c * size : (c + 1) * size, :] = lse
        else:
            lses[c * size : (c + 1) * size, :] = lse
    if not own:
        count = cdiv(rows, HD)
        eye = lax.broadcasted_iota(jnp.int32, (HD, HD), 0) == lax.broadcasted_iota(
            jnp.int32, (HD, HD), 1
        )
        if count * HD > rows:
            lses[rows:, :] = jnp.zeros((count * HD - rows, HD), jnp.float32)
        lines = [
            jnp.sum(jnp.where(eye, lses[b * HD : (b + 1) * HD, :], 0.0), axis=0, keepdims=True)
            for b in range(count)
        ]
        line = jnp.concatenate(lines, axis=0)
        high = line.astype(jnp.bfloat16)
        rest_1 = line - high.astype(jnp.float32)
        middle = rest_1.astype(jnp.bfloat16)
        low = (rest_1 - middle.astype(jnp.float32)).astype(jnp.bfloat16)
        stats = jnp.concatenate(
            [high.astype(jnp.float32), middle.astype(jnp.float32), low.astype(jnp.float32)], axis=0
        )
        pad = o_ref.shape[0] - rows - 3 * count
        if pad:
            stats = jnp.concatenate([stats, jnp.zeros((pad, HD), jnp.float32)], axis=0)
        o_ref[rows:, :] = stats.astype(jnp.bfloat16)


def combine_kernel(others, rows, *refs):
    received = refs[:others]
    o_ref, lse_ref, out_ref = refs[others:]
    count = cdiv(rows, HD)
    eye = lax.broadcasted_iota(jnp.int32, (HD, HD), 0) == lax.broadcasted_iota(
        jnp.int32, (HD, HD), 1
    )
    stats = []
    for ref in received:
        s = ref[rows:, :].astype(jnp.float32)
        stats.append(s[:count] + s[count : 2 * count] + s[2 * count : 3 * count])
    for b in range(count):
        size = min(HD, rows - b * HD)
        part = slice(b * HD, b * HD + size)
        all_lse = [lse_ref[part, :]]
        for s in stats:
            line = jnp.where(eye[:size], jnp.broadcast_to(s[b : b + 1], (size, HD)), 0.0)
            all_lse.append(lanes(jnp.sum(line, axis=1, keepdims=True)))
        top = functools.reduce(jnp.maximum, all_lse)
        weight = jnp.exp2(all_lse[0] - top)
        total = weight
        acc = o_ref[part, :] * weight
        for ref, lse in zip(received, all_lse[1:]):
            weight = jnp.exp2(lse - top)
            total = total + weight
            acc = acc + ref[part, :].astype(jnp.float32) * weight
        out_ref[part, :] = (acc / total).astype(jnp.bfloat16)


def mix_kernel(aligned, partner, lower, a_ref, b_ref, g_ref, out_ref, buf):
    steps, row_dev, width = out_ref.shape
    share = width // HD
    per_row = steps * share
    scales = g_ref[...]
    scales = jnp.concatenate([scales] * steps, axis=0)
    for r in range(row_dev):
        mine = a_ref[r * per_row : (r + 1) * per_row, :].astype(jnp.float32)
        start = pl.multiple_of(partner[r] * per_row, per_row) if aligned else r * per_row
        other = b_ref[pl.ds(start, per_row), :].astype(jnp.float32)
        is_lower = lower[r] > 0
        cond = jnp.where(is_lower, mine, other)
        uncond = jnp.where(is_lower, other, mine)
        mix = uncond + scales * (cond - uncond)
        square = jnp.mean(mix * mix, axis=1, keepdims=True)
        buf[r * per_row : (r + 1) * per_row, :] = mix / jnp.sqrt(square + 1e-06)
    for t in range(steps):
        for g in range(share):
            out_ref[t, :, g * HD : (g + 1) * HD] = buf[
                pl.ds(t * share + g, row_dev, stride=per_row), :
            ].astype(jnp.bfloat16)


def shifted(value, axis, steps):
    count = lax.axis_size(axis)
    pairs = [(source, (source + steps) % count) for source in range(count)]
    return lax.ppermute(value, axis, pairs)


def local(
    queries,
    prefix_keys,
    prefix_values,
    suffix_keys,
    suffix_values,
    new_keys,
    new_values,
    lengths,
    pair_of,
    guidance,
):
    steps, row_dev, width = queries.shape
    positions, kv_width = prefix_keys.shape
    kv_heads = kv_width // HD
    heads = width // HD
    group = heads // kv_heads
    suf_dev = suffix_keys.shape[1]
    shards = lax.axis_size("seq")
    share = heads // shards
    rows = steps * row_dev * share
    count = cdiv(rows, HD)
    extra = cdiv(3 * count, 16) * 16
    me = lax.axis_index("seq")

    def meta(dest):
        return jnp.stack([dest, dest * share // group, me * suf_dev]).astype(jnp.int32)

    def partial(dest, own):
        in_specs = [
            pl.BlockSpec((steps, row_dev, share * HD), lambda i, m, n: (0, 0, m[0])),
            pl.BlockSpec((positions, HD), lambda i, m, n: (0, m[1])),
            pl.BlockSpec((positions, HD), lambda i, m, n: (0, m[1])),
            pl.BlockSpec((row_dev, suf_dev, HD), lambda i, m, n: (0, 0, m[1])),
            pl.BlockSpec((row_dev, suf_dev, HD), lambda i, m, n: (0, 0, m[1])),
        ]
        args = [queries, prefix_keys, prefix_values, suffix_keys, suffix_values]
        if own:
            in_specs += [pl.BlockSpec((steps, row_dev, HD), lambda i, m, n: (0, 0, m[1]))] * 2
            args += [new_keys, new_values]
            out_shape = (
                jax.ShapeDtypeStruct((rows, HD), jnp.float32),
                jax.ShapeDtypeStruct((rows, HD), jnp.float32),
            )
            out_specs = (
                pl.BlockSpec((rows, HD), lambda i, m, n: (0, 0)),
                pl.BlockSpec((rows, HD), lambda i, m, n: (0, 0)),
            )
        else:
            out_shape = jax.ShapeDtypeStruct((rows + extra, HD), jnp.bfloat16)
            out_specs = pl.BlockSpec((rows + extra, HD), lambda i, m, n: (0, 0))
        return pl.pallas_call(
            functools.partial(partial_kernel, own, 4),
            grid_spec=pltpu.PrefetchScalarGridSpec(
                num_scalar_prefetch=2,
                grid=(1,),
                in_specs=in_specs,
                out_specs=out_specs,
                scratch_shapes=[
                    pltpu.VMEM((rows, HD), jnp.float32),
                    pltpu.VMEM((count * HD, HD), jnp.float32),
                ],
            ),
            out_shape=out_shape,
            cost_estimate=pl.CostEstimate(
                flops=4 * rows * positions * HD,
                bytes_accessed=4 * positions * HD + 4 * row_dev * suf_dev * HD,
                transcendentals=rows * positions,
            ),
            name="own" if own else "partial",
        )(meta(dest), lengths, *args)

    order = sorted(range(1, shards), key=lambda j: -min(j, shards - j))
    received = []
    for j in order:
        out = partial((me + j) % shards, False)
        received.append(shifted(out, "seq", j))
    own_out, own_lse = partial(me, True)
    attention = pl.pallas_call(
        functools.partial(combine_kernel, shards - 1, rows),
        out_shape=jax.ShapeDtypeStruct((rows, HD), jnp.bfloat16),
        name="combine",
    )(*received, own_out, own_lse)

    mine = lax.axis_index("row") * row_dev + jnp.arange(row_dev, dtype=jnp.int32)
    partner = lax.dynamic_slice_in_dim(pair_of, lax.axis_index("row") * row_dev, row_dev, 0)
    across = shifted(attention, "row", lax.axis_size("row") // 2)
    scales = lax.dynamic_slice_in_dim(guidance, me * share, share, 0)
    aligned = (steps * share) % 16 == 0
    if not aligned:
        across = jnp.take(across.reshape(row_dev, -1, HD), partner % row_dev, axis=0)
        across = across.reshape(rows, HD)
    return pl.pallas_call(
        functools.partial(mix_kernel, aligned),
        grid_spec=pltpu.PrefetchScalarGridSpec(
            num_scalar_prefetch=2,
            grid=(1,),
            in_specs=[
                pl.BlockSpec((rows, HD), lambda i, m, n: (0, 0)),
                pl.BlockSpec((rows, HD), lambda i, m, n: (0, 0)),
                pl.BlockSpec((share, HD), lambda i, m, n: (0, 0)),
            ],
            out_specs=pl.BlockSpec((steps, row_dev, share * HD), lambda i, m, n: (0, 0, 0)),
            scratch_shapes=[pltpu.VMEM((rows, HD), jnp.float32)],
        ),
        out_shape=jax.ShapeDtypeStruct((steps, row_dev, share * HD), jnp.bfloat16),
        name="mix",
    )(
        partner % row_dev,
        (mine < partner).astype(jnp.int32),
        attention,
        across,
        jnp.broadcast_to(scales[:, None], (share, HD)),
    )


def solution(mesh):
    placed = (
        P(None, "row", None),
        P("seq", None),
        P("seq", None),
        P("row", "seq", None),
        P("row", "seq", None),
        P(None, "row", None),
        P(None, "row", None),
        P("row"),
        P(),
        P(),
    )
    return jax.shard_map(
        local, mesh=mesh, in_specs=placed, out_specs=P(None, "row", "seq"), check_vma=False
    )
```

time: 111 us -> 48.2 us (0.43)
  waiting for transfers between devices: 36.8 us -> 3.26 us
  Pallas kernels: 0 us -> 29.8 us
  matrix products: 22.2 us -> 0 us
  local copies, waits for them, and re-layouts: 17.6 us -> 1.56 us
  other arithmetic: 16.7 us -> 3.77 us
  starting transfers between devices: 16.6 us -> 9.4 us
    all_to_all x3 -> x0, waiting for transfers between devices: 32.4 us -> none  [the longest x1 30.4 us: local(): lax.all_to_all(summed[None], 'seq', split_axis=3, concat_axis=0, tiled=True)]
    pallas_call x0 -> x6, Pallas kernels: none -> 29.8 us  [the longest x4 24.5 us: partial(): pl.pallas_call(functools.partial(partial_kernel, own, 4), grid_spec=pltpu...]
    dot_general x6 -> x0, matrix products: 22.2 us -> none  [the longest x1 8.05 us: local(): jnp.einsum('trkgn,nkd->trkgd', pre_weights.astype(jnp.bfloat16), pre_valu...]
    all_to_all x3 -> x0, starting transfers between devices: 15 us -> none  [the longest x1 6.34 us: local(): lax.all_to_all(total[None], 'seq', split_axis=3, concat_axis=0, tiled=True)]
    reduce_sum x6 -> x0, other arithmetic: 12.3 us -> none  [the longest x2 11.2 us: local(): total = jnp.sum(pre_weights, -1) + jnp.sum(suf_weights, -1)]
    ppermute x1 -> x4, starting transfers between devices: 1.58 us -> 9.4 us  [shifted(): return lax.ppermute(value, axis, pairs)]
    reshape x7 -> x0, local copies, waits for them, and re-layouts: 6.29 us -> none  [the longest x1 2.36 us: local(): pre_keys = prefix_keys.reshape(-1, kv_heads, HD)]
    unnamed x26 -> x12, local copies, waits for them, and re-layouts: 3.91 us -> 0.8 us
  transfers between devices with their start and end apart: 4 -> 4, of which waited for: 3 -> 1; matrix products, arithmetic and copies ran while one was open for 23% -> 7% of each run, Pallas kernels for 0% -> 39%
where the time goes in v1:
time: 48.2 us; the launch traced here: 47.9 us
  Pallas kernels  29.8 us (62%)
  starting transfers between devices  9.4 us (20%)
  other arithmetic  3.77 us (8%)
  waiting for transfers between devices  3.26 us (7%)
  local copies, waits for them, and re-layouts  1.56 us (3%)
    pallas_call x4, Pallas kernels, partial(): pl.pallas_call(functools.partial(partial_kernel, own, 4), grid_spec=pltpu...  24.5 us
    ppermute x4, starting transfers between devices, shifted(): return lax.ppermute(value, axis, pairs)  9.4 us
    ppermute x4, waiting for transfers between devices, shifted(): return lax.ppermute(value, axis, pairs)  3.26 us
    pallas_call x1, Pallas kernels, local(): pl.pallas_call(functools.partial(mix_kernel, aligned), grid_spec=pltpu.Pr...  2.76 us
    pallas_call x1, Pallas kernels, local(): pl.pallas_call(functools.partial(combine_kernel, shards - 1, rows), out_s...  2.54 us
    another operation x4, other arithmetic, meta(): jnp.stack([dest, dest * share // group, me * suf_dev]).astype(jnp.int32)  2.52 us
  transfers between devices with their start and end apart: 4, of which 1 were waited for; matrix products, arithmetic and copies ran while one was open for 7% of the time, Pallas kernels for 39%

profile of v1, /device:TPU:0, one launch (start us, length us, event | category | flops | bytes accessed | tf_op | source)
XLA Modules:
  0.0 47.9 jit_solution(1709971620868468373)
XLA Ops:
  0.0 0.6 %add_add_fusion.meta = s32[3]{0:T(128)} fusion(s32[1]{0:T(128)} %bitcast.1, s32[1]{0:T(128)} %bitcast, s32[1]{0:T(128)} %bitcast.2), kind=kLoop, calls=%fused_computation.5 | loop fusion | flops 6 | bytes 24 | tf_op jit(solution)/shard_map/stack | solution.py:223
  0.6 6.0 %partial.3 = bf16[800,128]{1,0:T(8,128)(2,1)} custom-call(s32[3]{0:T(128)} %add_add_fusion.meta, s32[16]{0:T(128)} %lengths.7, bf16[3,16,8192]{2,1,0:T(8,128)(2,1)} %q_ref.7, bf16[1536,512]{1,0:T(8,128)(2,1)} %k_ref.7, bf16[1536,512]{1,0:T(8,128)(2,1)} %v_ref.7, bf16[16,64,512]{2,1,0:T(8,128)(2,1)} %sk_ref.7, bf16[16,64,512]{2,1,0:T(8,128)(2,1)} %sv_ref.7), custom_call_target="tpu_custom_call" | custom-call | flops 603979776 | bytes 1310720 | tf_op jit(solution)/shard_map/partial/pallas_call | solution.py:248
  6.6 4.1 %collective-permute-start = (bf16[800,128]{1,0:T(8,128)(2,1)}, bf16[800,128]{1,0:T(8,128)(2,1)S(1)}, u32[]{:S(2)}, u32[]{:S(2)}) collective-permute-start(bf16[800,128]{1,0:T(8,128)(2,1)} %partial.3), channel_id=1, source_target_pairs={{0,16},{8,24},{16,0},{24,8},{1,17},{9,25},{17,1},{25,9},{2,18},{10... | collective-permute-start | bytes 614408 | tf_op jit(solution)/shard_map/ppermute | solution.py:194
  10.7 0.7 %add_add_fusion.1.meta = s32[3]{0:T(128)} fusion(s32[1]{0:T(128)} %bitcast.4, s32[1]{0:T(128)} %bitcast.3, s32[1]{0:T(128)} %bitcast.2), kind=kLoop, calls=%fused_computation.6 | loop fusion | flops 6 | bytes 24 | tf_op jit(solution)/shard_map/stack | solution.py:223
  11.3 6.0 %partial.4 = bf16[800,128]{1,0:T(8,128)(2,1)} custom-call(s32[3]{0:T(128)} %add_add_fusion.1.meta, s32[16]{0:T(128)} %lengths.7, bf16[3,16,8192]{2,1,0:T(8,128)(2,1)} %q_ref.7, bf16[1536,512]{1,0:T(8,128)(2,1)} %k_ref.7, bf16[1536,512]{1,0:T(8,128)(2,1)} %v_ref.7, bf16[16,64,512]{2,1,0:T(8,128)(2,1)} %sk_ref.7, bf16[16,64,512]{2,1,0:T(8,128)(2,1)} %sv_ref.7), custom_call_target="tpu_custom_call" | custom-call | flops 603979776 | bytes 1310720 | tf_op jit(solution)/shard_map/partial/pallas_call | solution.py:248
  17.4 1.6 %collective-permute-start.1 = (bf16[800,128]{1,0:T(8,128)(2,1)}, bf16[800,128]{1,0:T(8,128)(2,1)S(1)}, u32[]{:S(2)}, u32[]{:S(2)}) collective-permute-start(bf16[800,128]{1,0:T(8,128)(2,1)} %partial.4), channel_id=1, source_target_pairs={{0,8},{8,16},{16,24},{24,0},{1,9},{9,17},{17,25},{25,1},{2,10},{10... | collective-permute-start | bytes 614408 | tf_op jit(solution)/shard_map/ppermute | solution.py:194
  18.9 0.7 %add_add_fusion.2.meta = s32[3]{0:T(128)} fusion(s32[1]{0:T(128)} %bitcast.6, s32[1]{0:T(128)} %bitcast.5, s32[1]{0:T(128)} %bitcast.2), kind=kLoop, calls=%fused_computation.7 | loop fusion | flops 6 | bytes 24 | tf_op jit(solution)/shard_map/stack | solution.py:223
  19.6 0.0 copy-start.5
  19.6 6.2 %partial.5 = bf16[800,128]{1,0:T(8,128)(2,1)} custom-call(s32[3]{0:T(128)} %add_add_fusion.2.meta, s32[16]{0:T(128)} %lengths.7, bf16[3,16,8192]{2,1,0:T(8,128)(2,1)} %q_ref.7, bf16[1536,512]{1,0:T(8,128)(2,1)} %k_ref.7, bf16[1536,512]{1,0:T(8,128)(2,1)} %v_ref.7, bf16[16,64,512]{2,1,0:T(8,128)(2,1)} %sk_ref.7, bf16[16,64,512]{2,1,0:T(8,128)(2,1)} %sv_ref.7), custom_call_target="tpu_custom_call" | custom-call | flops 603979776 | bytes 1310720 | tf_op jit(solution)/shard_map/partial/pallas_call | solution.py:248
  25.8 2.2 %collective-permute-start.2 = (bf16[800,128]{1,0:T(8,128)(2,1)}, bf16[800,128]{1,0:T(8,128)(2,1)S(1)}, u32[]{:S(2)}, u32[]{:S(2)}) collective-permute-start(bf16[800,128]{1,0:T(8,128)(2,1)} %partial.5), channel_id=1, source_target_pairs={{0,24},{8,0},{16,8},{24,16},{1,25},{9,1},{17,9},{25,17},{2,26},{10... | collective-permute-start | bytes 614408 | tf_op jit(solution)/shard_map/ppermute | solution.py:194
  28.0 0.0 copy-done.5
  28.0 0.1 dynamic_slice.7
  28.1 0.6 %add_add_fusion.3.meta = s32[3]{0:T(128)} fusion(s32[1]{0:T(128)} %bitcast.8, s32[1]{0:T(128)} %bitcast.7, s32[1]{0:T(128)} %bitcast.2), kind=kLoop, calls=%fused_computation.8 | loop fusion | flops 6 | bytes 24 | tf_op jit(solution)/shard_map/stack | solution.py:223
  28.7 6.3 %own.1 = (f32[768,128]{1,0:T(8,128)}, f32[768,128]{1,0:T(8,128)}) custom-call(s32[3]{0:T(128)} %add_add_fusion.3.meta, s32[16]{0:T(128)} %lengths.7, bf16[3,16,8192]{2,1,0:T(8,128)(2,1)} %q_ref.7, bf16[1536,512]{1,0:T(8,128)(2,1)} %k_ref.7, bf16[1536,512]{1,0:T(8,128)(2,1)} %v_ref.7, bf16[16,64,512]{2,1,0:T(8,128)(2,1)} %sk_ref.7, ...), custom_call_target="tpu_custom_call" | custom-call | flops 603979776 | bytes 1310720 | tf_op jit(solution)/shard_map/own/pallas_call | solution.py:248
  35.0 0.0 copy-start.4
  35.0 0.0 collective-permute-done.refs_0_
  35.0 0.0 collective-permute-done.1.refs_1_
  35.0 0.0 copy-start.1
  35.1 0.0 collective-permute-done.2.refs_2_
  35.1 0.0 copy-start.2
  35.1 0.6 %copy-done = bf16[800,128]{1,0:T(8,128)(2,1)} copy-done((bf16[800,128]{1,0:T(8,128)(2,1)}, bf16[800,128]{1,0:T(8,128)(2,1)S(1)}, u32[]{:S(2)}) %copy-start) | copy-done | bytes 204824
  35.7 0.1 copy-done.1
  35.8 0.1 copy-done.2
  35.9 2.5 %combine.1.a_ref = bf16[768,128]{1,0:T(8,128)(2,1)} custom-call(bf16[800,128]{1,0:T(8,128)(2,1)} %copy-done, bf16[800,128]{1,0:T(8,128)(2,1)} %copy-done.1, bf16[800,128]{1,0:T(8,128)(2,1)} %copy-done.2, f32[768,128]{1,0:T(8,128)} %get-tuple-element.7.refs_3_, f32[768,128]{1,0:T(8,128)} %get-tuple-element.8.refs_4_), custom_call_target="tpu_custom_call" | custom-call | tf_op jit(solution)/shard_map/combine/pallas_call | solution.py:275
  38.4 1.5 %collective-permute-start.3 = (bf16[768,128]{1,0:T(8,128)(2,1)}, bf16[768,128]{1,0:T(8,128)(2,1)S(1)}, u32[]{:S(2)}, u32[]{:S(2)}) collective-permute-start(bf16[768,128]{1,0:T(8,128)(2,1)} %combine.1.a_ref), channel_id=1, source_target_pairs={{0,4},{1,5},{2,6},{3,7},{4,0},{5,1},{6,2},{7,3},{8,12},{9,13},{10,... | collective-permute-start | bytes 589832 | tf_op jit(solution)/shard_map/ppermute | solution.py:194
  39.9 0.0 copy-done.4
  39.9 0.7 %and_select_fusion.partner = s32[16]{0:T(128)} fusion(s32[128]{0:T(128)S(1)} %copy-done.4, s32[]{:T(128)S(6)} %select_n.40), kind=kLoop, calls=%fused_computation.3 | loop fusion | flops 176 | bytes 132 | tf_op jit(solution)/shard_map/jit(remainder)/select_n | solution.py:305
  40.6 0.6 %compare_convert_fusion.lower = s32[16]{0:T(128)} fusion(s32[]{:T(128)S(6)} %mul.23, s32[128]{0:T(128)S(1)} %copy-done.4, s32[]{:T(128)S(6)} %select_n.40), kind=kLoop, calls=%fused_computation.2 | loop fusion | flops 48 | bytes 136 | tf_op jit(solution)/shard_map/convert_element_type | solution.py:306
  41.2 3.3 %collective-permute-done.3.b_ref = bf16[768,128]{1,0:T(8,128)(2,1)S(1)} collective-permute-done((bf16[768,128]{1,0:T(8,128)(2,1)}, bf16[768,128]{1,0:T(8,128)(2,1)S(1)}, u32[]{:S(2)}, u32[]{:S(2)}) %collective-permute-start.3) | collective-permute-done | bytes 196640 | tf_op jit(solution)/shard_map/ppermute | solution.py:194
  44.4 0.7 %broadcast_in_dim.2.g_ref = f32[16,128]{1,0:T(8,128)} broadcast(f32[16]{0:T(128)S(1)} %dynamic_slice.7), dimensions={0} | broadcast | bytes 8256 | tf_op jit(solution)/shard_map/broadcast_in_dim | solution.py:309
  45.1 0.0 copy-done.3
  45.1 2.8 %mix.1 = bf16[3,16,2048]{2,1,0:T(8,128)(2,1)} custom-call(s32[16]{0:T(128)} %and_select_fusion.partner, s32[16]{0:T(128)} %compare_convert_fusion.lower, bf16[768,128]{1,0:T(8,128)(2,1)} %combine.1.a_ref, bf16[768,128]{1,0:T(8,128)(2,1)} %copy-done.3, f32[16,128]{1,0:T(8,128)} %broadcast_in_dim.2.g_ref), custom_call_target="tpu_custom_call" | custom-call | tf_op jit(solution)/shard_map/mix/pallas_call | solution.py:289
  (2 shorter events, 0.0 us)
Async XLA Ops:
  6.6 28.4 %collective-permute-start = (bf16[800,128]{1,0:T(8,128)(2,1)}, bf16[800,128]{1,0:T(8,128)(2,1)S(1)}, u32[]{:S(2)}, u32[]{:S(2)}) collective-permute-start(bf16[800,128]{1,0:T(8,128)(2,1)} %partial.3), channel_id=1, source_target_pairs={{0,16},{8,24},{16,0},{24,8},{1,17},{9,25},{17,1},{25,9},{2,18},{10... | collective-permute-start | bytes 614408 | tf_op jit(solution)/shard_map/ppermute | solution.py:194
  17.4 17.7 %collective-permute-start.1 = (bf16[800,128]{1,0:T(8,128)(2,1)}, bf16[800,128]{1,0:T(8,128)(2,1)S(1)}, u32[]{:S(2)}, u32[]{:S(2)}) collective-permute-start(bf16[800,128]{1,0:T(8,128)(2,1)} %partial.4), channel_id=1, source_target_pairs={{0,8},{8,16},{16,24},{24,0},{1,9},{9,17},{17,25},{25,1},{2,10},{10... | collective-permute-start | bytes 614408 | tf_op jit(solution)/shard_map/ppermute | solution.py:194
  19.6 8.4 %copy-start.5 = (f32[64]{0:T(128)S(1)}, f32[64]{0:T(128)}, u32[]{:S(2)}) copy-start(f32[64]{0:T(128)} %param.19) | copy-start | bytes 772
  25.8 9.3 %collective-permute-start.2 = (bf16[800,128]{1,0:T(8,128)(2,1)}, bf16[800,128]{1,0:T(8,128)(2,1)S(1)}, u32[]{:S(2)}, u32[]{:S(2)}) collective-permute-start(bf16[800,128]{1,0:T(8,128)(2,1)} %partial.5), channel_id=1, source_target_pairs={{0,24},{8,0},{16,8},{24,16},{1,25},{9,1},{17,9},{25,17},{2,26},{10... | collective-permute-start | bytes 614408 | tf_op jit(solution)/shard_map/ppermute | solution.py:194
  35.0 4.9 %copy-start.4 = (s32[128]{0:T(128)S(1)}, s32[128]{0:T(128)}, u32[]{:S(2)}) copy-start(s32[128]{0:T(128)} %param.18) | copy-start | bytes 1540
  35.0 0.7 %copy-start = (bf16[800,128]{1,0:T(8,128)(2,1)}, bf16[800,128]{1,0:T(8,128)(2,1)S(1)}, u32[]{:S(2)}) copy-start(bf16[800,128]{1,0:T(8,128)(2,1)S(1)} %collective-permute-done.refs_0_) | copy-start | bytes 614404
  35.0 0.7 %copy-start.1 = (bf16[800,128]{1,0:T(8,128)(2,1)}, bf16[800,128]{1,0:T(8,128)(2,1)S(1)}, u32[]{:S(2)}) copy-start(bf16[800,128]{1,0:T(8,128)(2,1)S(1)} %collective-permute-done.1.refs_1_) | copy-start | bytes 614404
  35.1 0.8 %copy-start.2 = (bf16[800,128]{1,0:T(8,128)(2,1)}, bf16[800,128]{1,0:T(8,128)(2,1)S(1)}, u32[]{:S(2)}) copy-start(bf16[800,128]{1,0:T(8,128)(2,1)S(1)} %collective-permute-done.2.refs_2_) | copy-start | bytes 614404
  38.4 6.0 %collective-permute-start.3 = (bf16[768,128]{1,0:T(8,128)(2,1)}, bf16[768,128]{1,0:T(8,128)(2,1)S(1)}, u32[]{:S(2)}, u32[]{:S(2)}) collective-permute-start(bf16[768,128]{1,0:T(8,128)(2,1)} %combine.1.a_ref), channel_id=1, source_target_pairs={{0,4},{1,5},{2,6},{3,7},{4,0},{5,1},{6,2},{7,3},{8,12},{9,13},{10,... | collective-permute-start | bytes 589832 | tf_op jit(solution)/shard_map/ppermute | solution.py:194
  44.4 0.7 %copy-start.3 = (bf16[768,128]{1,0:T(8,128)(2,1)}, bf16[768,128]{1,0:T(8,128)(2,1)S(1)}, u32[]{:S(2)}) copy-start(bf16[768,128]{1,0:T(8,128)(2,1)S(1)} %collective-permute-done.3.b_ref) | copy-start | bytes 589828

commit v2 on v0

v2 whole, which is shorter than its diff:
```python
import functools

import jax
import jax.numpy as jnp
from jax import lax
from jax.experimental import pallas as pl
from jax.experimental.pallas import tpu as pltpu
from jax.sharding import PartitionSpec as P

HD = 128
LOG2E = 1.4426950408889634
NEG = -1e30
CHUNK = 4
MIB = 1 << 20
VMEM = pl.BlockSpec(memory_space=pltpu.VMEM)
SMEM = pl.BlockSpec(memory_space=pltpu.SMEM)
HBM = pl.BlockSpec(memory_space=pltpu.HBM)
PIECES = 2


def dot_nt(a, b):
    return lax.dot_general(a, b, (((1,), (1,)), ((), ())), preferred_element_type=jnp.float32)


def dot_nn(a, b):
    return lax.dot_general(a, b, (((1,), (0,)), ((), ())), preferred_element_type=jnp.float32)


def cdiv(a, b):
    return -(-a // b)


def lanes(x):
    return jnp.broadcast_to(x, (x.shape[0], HD))


def with_ones(values):
    return jnp.concatenate([values, jnp.ones_like(values)], axis=1)


def diagonal():
    shape = (HD, HD)
    return lax.broadcasted_iota(jnp.int32, shape, 0) == lax.broadcasted_iota(jnp.int32, shape, 1)


def attend(base, share, lengths, q_ref, k_ref, v_ref, sk_ref, sv_ref, fresh, qs, lses, emit, waits):
    steps, row_dev, _ = q_ref.shape
    per_row = steps * share
    suf_dev = sk_ref.shape[1]
    scale = HD ** (-0.5) * LOG2E
    waits[0]()
    for t in range(steps):
        for g in range(share):
            qs[pl.ds(t * share + g, row_dev, stride=per_row), :] = q_ref[
                t, :, g * HD : (g + 1) * HD
            ].astype(jnp.float32)
    waits[1]()
    keys = k_ref[...]
    size = CHUNK * per_row
    chunks = row_dev // CHUNK

    def scores(c):
        q = qs[c * size : (c + 1) * size, :].astype(jnp.bfloat16)
        parts = [dot_nt(q, keys)]
        suf = []
        for p in range(CHUNK // 2):
            r = c * CHUNK + 2 * p
            sk = sk_ref[r : r + 2].reshape(2 * suf_dev, HD)
            s = dot_nt(q[p * 2 * per_row : (p + 1) * 2 * per_row], sk)
            lane = lax.broadcasted_iota(jnp.int32, s.shape, 1)
            second = lax.broadcasted_iota(jnp.int32, s.shape, 0) >= per_row
            live0 = jnp.clip(lengths[r] - base, 0, suf_dev)
            live1 = jnp.clip(lengths[r + 1] - base, 0, suf_dev)
            low = jnp.where(second, suf_dev, 0)
            high = jnp.where(second, suf_dev + live1, live0)
            suf.append(jnp.where((lane >= low) & (lane < high), s, NEG))
        parts.append(jnp.concatenate(suf, axis=0))
        if fresh is not None:
            s = dot_nt(q, fresh[0])
            row = lax.broadcasted_iota(jnp.int32, s.shape, 0)
            col = lax.broadcasted_iota(jnp.int32, s.shape, 1)
            same = (col % row_dev) == (c * CHUNK + row // per_row)
            causal = (col // row_dev) <= ((row % per_row) // share)
            parts.append(jnp.where(same & causal, s, NEG))
        return parts

    ahead = scores(0)
    waits[2]()
    values = with_ones(v_ref[...])
    for c in range(chunks):
        parts = ahead
        if c + 1 < chunks:
            ahead = scores(c + 1)
        top = jnp.max(parts[0], axis=1, keepdims=True)
        for s in parts[1:]:
            top = jnp.maximum(top, jnp.max(s, axis=1, keepdims=True))
        weights = [jnp.exp2((s - top) * scale).astype(jnp.bfloat16) for s in parts]
        acc = dot_nn(weights[0], values)
        suf = []
        for p in range(CHUNK // 2):
            r = c * CHUNK + 2 * p
            sv = with_ones(sv_ref[r : r + 2].reshape(2 * suf_dev, HD))
            suf.append(dot_nn(weights[1][p * 2 * per_row : (p + 1) * 2 * per_row], sv))
        acc = acc + jnp.concatenate(suf, axis=0)
        if fresh is not None:
            acc = acc + dot_nn(weights[2], fresh[1])
        total = acc[:, HD:]
        part = slice(c * size, (c + 1) * size)
        emit(part, acc[:, :HD] / total)
        lses[part, :] = lanes(top * scale) + jnp.log2(total)


def stat_lines(lses, rows):
    count = cdiv(rows, HD)
    eye = diagonal()
    if count * HD > rows:
        lses[rows:, :] = jnp.zeros((count * HD - rows, HD), jnp.float32)
    lines = [
        jnp.sum(jnp.where(eye, lses[b * HD : (b + 1) * HD, :], 0.0), axis=0, keepdims=True)
        for b in range(count)
    ]
    return jnp.concatenate(lines, axis=0)


def slabs(dest, share, group, state):
    q_ref, k_ref, v_ref, sk_ref, sv_ref = state
    q_at = pl.multiple_of(dest * (share * HD), HD)
    kv_at = pl.multiple_of((dest * share // group) * HD, HD)
    q_lanes, kv_lanes = pl.ds(q_at, share * HD), pl.ds(kv_at, HD)
    return (
        q_ref.at[:, :, q_lanes],
        k_ref.at[:, kv_lanes],
        v_ref.at[:, kv_lanes],
        sk_ref.at[:, :, kv_lanes],
        sv_ref.at[:, :, kv_lanes],
    )


def copies_of(sources, targets, sems):
    out = []
    for i, (source, target) in enumerate(zip(sources, targets)):
        n = source.shape[0]
        pieces = PIECES if i and n % (16 * PIECES) == 0 else 1
        step = n // pieces
        out.append(
            [
                pltpu.make_async_copy(
                    source.at[pl.ds(p * step, step)],
                    target.at[pl.ds(p * step, step)],
                    sems.at[i, p],
                )
                for p in range(pieces)
            ]
        )
    return out


def start(copies):
    for copy in copies:
        copy.start()


def wait(*lists):
    for copies in lists:
        for copy in copies:
            copy.wait()


def send_kernel(share, shifts, group, lengths, *refs):
    state, refs = refs[:5], refs[5:]
    me = lax.axis_index("seq")
    count = lax.axis_size("seq")
    base = me * state[3].shape[1]
    here, later = [lax.rem(me + s, count) for s in shifts]
    now = None
    if len(refs) == 17:
        o_ref, ahead, qs, lses, buffers = refs[0], refs[1:6], refs[6], refs[7], refs[8:13]
        spot, sems, next_sems, spot_sem = refs[13:]
        now = copies_of(slabs(here, share, group, state), buffers, sems)
        size = pltpu.make_async_copy(lengths, spot, spot_sem)
        lengths = spot
        size.start()
        for i in (0, 1, 3, 2, 4):
            start(now[i])
    else:
        buffers, o_ref, ahead, qs, lses, next_sems = refs[:5], refs[5], refs[6:11], refs[11], refs[12], refs[13]
    after = copies_of(slabs(later, share, group, state), ahead, next_sems)

    def fetch():
        for copies in after:
            start(copies)

    if now is None:
        fetch()
        waits = [lambda: None] * 3
    else:

        def wait_keys():
            wait(now[1], now[3])
            size.wait()

        def wait_values():
            wait(now[2], now[4])
            fetch()

        waits = [lambda: wait(now[0]), wait_keys, wait_values]
    rows = qs.shape[0]

    def emit(part, out):
        o_ref[part, :] = out.astype(jnp.bfloat16)

    attend(base, share, lengths, *buffers, None, qs, lses, emit, waits)
    line = stat_lines(lses, rows)
    high = line.astype(jnp.bfloat16).astype(jnp.float32)
    rest = line - high
    middle = rest.astype(jnp.bfloat16).astype(jnp.float32)
    stats = [high, middle, rest - middle]
    pad = o_ref.shape[0] - rows - 3 * line.shape[0]
    if pad:
        stats.append(jnp.zeros((pad, HD), jnp.float32))
    o_ref[rows:, :] = jnp.concatenate(stats, axis=0).astype(jnp.bfloat16)
    wait(*after)


def own_kernel(share, group, lengths, *refs):
    buffers, (nk_ref, nv_ref, o_ref, line_ref, qs, lses) = refs[:5], refs[5:]
    steps, row_dev = nk_ref.shape[:2]
    rows = qs.shape[0]
    me = lax.axis_index("seq")
    kv_lanes = pl.ds(pl.multiple_of((me * share // group) * HD, HD), HD)
    new_keys = nk_ref[:, :, kv_lanes].reshape(steps * row_dev, HD)
    new_values = with_ones(nv_ref[:, :, kv_lanes].reshape(steps * row_dev, HD))

    def emit(part, out):
        o_ref[part, :] = out

    base = me * buffers[3].shape[1]
    waits = [lambda: None] * 3
    attend(base, share, lengths, *buffers, (new_keys, new_values), qs, lses, emit, waits)
    line = stat_lines(lses, rows)
    line_ref[: line.shape[0], :] = line


def combine_kernel(others, *refs):
    received = refs[:others]
    o_ref, line_ref, out_ref = refs[others:]
    rows = o_ref.shape[0]
    count = cdiv(rows, HD)
    lines = [line_ref[:count, :]]
    for ref in received:
        s = ref[rows:, :].astype(jnp.float32)
        lines.append(s[:count] + s[count : 2 * count] + s[2 * count : 3 * count])
    top = functools.reduce(jnp.maximum, lines)
    weights = [jnp.exp2(s - top) for s in lines]
    total = functools.reduce(jnp.add, weights)
    table = jnp.concatenate([w / total for w in weights], axis=0)
    height = cdiv(table.shape[0], HD) * HD
    table = jnp.concatenate([table, jnp.zeros((height - table.shape[0], HD), jnp.float32)], axis=0)
    table = table.T
    for b in range(count):
        size = min(HD, rows - b * HD)
        part = slice(b * HD, b * HD + size)
        acc = o_ref[part, :] * lanes(table[:size, b : b + 1])
        for i, ref in enumerate(received):
            at = (i + 1) * count + b
            acc = acc + ref[part, :].astype(jnp.float32) * lanes(table[:size, at : at + 1])
        out_ref[part, :] = acc.astype(jnp.bfloat16)


def mix_kernel(aligned, pair_of, guidance, a_ref, b_ref, out_ref, buf):
    steps, row_dev, width = out_ref.shape
    share = width // HD
    per_row = steps * share
    head = lax.axis_index("seq") * share
    first = lax.axis_index("row") * row_dev
    index = lax.broadcasted_iota(jnp.int32, (share, HD), 0)
    scales = jnp.zeros((share, HD), jnp.float32)
    for g in range(share):
        scales = jnp.where(index == g, guidance[head + g], scales)
    scales = jnp.concatenate([scales] * steps, axis=0)
    for r in range(row_dev):
        partner = pair_of[first + r]
        mine = a_ref[r * per_row : (r + 1) * per_row, :].astype(jnp.float32)
        if aligned:
            start = pl.multiple_of(lax.rem(partner, row_dev) * per_row, per_row)
        else:
            start = r * per_row
        other = b_ref[pl.ds(start, per_row), :].astype(jnp.float32)
        is_lower = first + r < partner
        cond = jnp.where(is_lower, mine, other)
        uncond = jnp.where(is_lower, other, mine)
        mix = uncond + scales * (cond - uncond)
        square = jnp.mean(mix * mix, axis=1, keepdims=True)
        buf[r * per_row : (r + 1) * per_row, :] = mix / jnp.sqrt(square + 1e-06)
    for t in range(steps):
        for g in range(share):
            out_ref[t, :, g * HD : (g + 1) * HD] = buf[
                pl.ds(t * share + g, row_dev, stride=per_row), :
            ].astype(jnp.bfloat16)


def shifted(value, axis, steps):
    count = lax.axis_size(axis)
    pairs = [(source, (source + steps) % count) for source in range(count)]
    return lax.ppermute(value, axis, pairs)


def local(
    queries,
    prefix_keys,
    prefix_values,
    suffix_keys,
    suffix_values,
    new_keys,
    new_values,
    lengths,
    pair_of,
    guidance,
):
    steps, row_dev, width = queries.shape
    positions, kv_width = prefix_keys.shape
    kv_heads = kv_width // HD
    heads = width // HD
    group = heads // kv_heads
    suf_dev = suffix_keys.shape[1]
    shards = lax.axis_size("seq")
    share = heads // shards
    rows = steps * row_dev * share
    count = cdiv(rows, HD)
    extra = cdiv(3 * count, 16) * 16
    work = [
        pltpu.VMEM((rows, HD), jnp.float32),
        pltpu.VMEM((count * HD, HD), jnp.float32),
    ]
    cost = pl.CostEstimate(
        flops=4 * rows * positions * HD,
        bytes_accessed=4 * positions * HD + 4 * row_dev * suf_dev * HD,
        transcendentals=rows * positions,
    )
    params = pltpu.CompilerParams(vmem_limit_bytes=24 * MIB)
    state = (queries, prefix_keys, prefix_values, suffix_keys, suffix_values)
    state = [pltpu.with_memory_space_constraint(x, pltpu.HBM) for x in state]
    fixed_lengths = pltpu.with_memory_space_constraint(lengths, pltpu.HBM)

    shapes = (
        (steps, row_dev, share * HD),
        (positions, HD),
        (positions, HD),
        (row_dev, suf_dev, HD),
        (row_dev, suf_dev, HD),
    )
    sems = pltpu.SemaphoreType.DMA((5, PIECES))

    def partial(shift, later, operands):
        first = operands is None
        scratch = list(work)
        if first:
            scratch += [pltpu.VMEM(shape, jnp.bfloat16) for shape in shapes]
            scratch += [pltpu.SMEM((row_dev,), jnp.int32), sems]
        scratch.append(sems)
        if first:
            scratch.append(pltpu.SemaphoreType.DMA)
        return pl.pallas_call(
            functools.partial(send_kernel, share, (shift, later), group),
            in_specs=[HBM if first else SMEM] + [HBM] * 5 + ([] if first else [VMEM] * 5),
            out_specs=[VMEM] * 6,
            scratch_shapes=scratch,
            out_shape=[jax.ShapeDtypeStruct((rows + extra, HD), jnp.bfloat16)]
            + [jax.ShapeDtypeStruct(shape, jnp.bfloat16) for shape in shapes],
            cost_estimate=cost,
            compiler_params=params,
            name="partial",
        )(fixed_lengths if first else lengths, *state, *(operands or ()))

    order = sorted(range(1, shards), key=lambda j: -min(j, shards - j))
    received = []
    operands = None
    for j, later in zip(order, order[1:] + [0]):
        out, *operands = partial(j, later, operands)
        received.append(shifted(out, "seq", j))
    own_out, own_line = pl.pallas_call(
        functools.partial(own_kernel, share, group),
        in_specs=[SMEM] + [VMEM] * 7,
        out_specs=(VMEM, VMEM),
        scratch_shapes=work,
        out_shape=(
            jax.ShapeDtypeStruct((rows, HD), jnp.float32),
            jax.ShapeDtypeStruct((cdiv(count, 8) * 8, HD), jnp.float32),
        ),
        cost_estimate=cost,
        compiler_params=params,
        name="own",
    )(lengths, *operands, new_keys, new_values)
    attention = pl.pallas_call(
        functools.partial(combine_kernel, shards - 1),
        in_specs=[VMEM] * (shards + 1),
        out_specs=VMEM,
        out_shape=jax.ShapeDtypeStruct((rows, HD), jnp.bfloat16),
        compiler_params=params,
        name="combine",
    )(*received, own_out, own_line)

    across = shifted(attention, "row", lax.axis_size("row") // 2)
    aligned = (steps * share) % 16 == 0
    if not aligned:
        partner = lax.dynamic_slice_in_dim(pair_of, lax.axis_index("row") * row_dev, row_dev, 0)
        across = jnp.take(across.reshape(row_dev, -1, HD), partner % row_dev, axis=0)
        across = across.reshape(rows, HD)
    return pl.pallas_call(
        functools.partial(mix_kernel, aligned),
        in_specs=[SMEM, SMEM, VMEM, VMEM],
        scratch_shapes=[pltpu.VMEM((rows, HD), jnp.float32)],
        out_specs=VMEM,
        out_shape=jax.ShapeDtypeStruct((steps, row_dev, share * HD), jnp.bfloat16),
        compiler_params=params,
        name="mix",
    )(pair_of, guidance, attention, across)


def solution(mesh):
    placed = (
        P(None, "row", None),
        P("seq", None),
        P("seq", None),
        P("row", "seq", None),
        P("row", "seq", None),
        P(None, "row", None),
        P(None, "row", None),
        P("row"),
        P(),
        P(),
    )
    return jax.shard_map(
        local, mesh=mesh, in_specs=placed, out_specs=P(None, "row", "seq"), check_vma=False
    )
```

time: 111 us -> 36.1 us (0.33)
  waiting for transfers between devices: 36.8 us -> 8.69 us
  matrix products: 22.2 us -> 0 us
  local copies, waits for them, and re-layouts: 17.6 us -> 0.02 us
  Pallas kernels: 0 us -> 17.4 us
  other arithmetic: 16.7 us -> 0 us
  starting transfers between devices: 16.6 us -> 9.69 us
    all_to_all x3 -> x0, waiting for transfers between devices: 32.4 us -> none  [the longest x1 30.4 us: local(): lax.all_to_all(summed[None], 'seq', split_axis=3, concat_axis=0, tiled=True)]
    dot_general x6 -> x0, matrix products: 22.2 us -> none  [the longest x1 8.05 us: local(): jnp.einsum('trkgn,nkd->trkgd', pre_weights.astype(jnp.bfloat16), pre_valu...]
    pallas_call x0 -> x6, Pallas kernels: none -> 17.4 us  [the longest x3 12.3 us: partial(): pl.pallas_call(functools.partial(send_kernel, share, (shift, later), grou...]
    all_to_all x3 -> x0, starting transfers between devices: 15 us -> none  [the longest x1 6.34 us: local(): lax.all_to_all(total[None], 'seq', split_axis=3, concat_axis=0, tiled=True)]
    reduce_sum x6 -> x0, other arithmetic: 12.3 us -> none  [the longest x2 11.2 us: local(): total = jnp.sum(pre_weights, -1) + jnp.sum(suf_weights, -1)]
    ppermute x1 -> x4, starting transfers between devices: 1.58 us -> 9.69 us  [shifted(): return lax.ppermute(value, axis, pairs)]
    reshape x7 -> x0, local copies, waits for them, and re-layouts: 6.29 us -> none  [the longest x1 2.36 us: local(): pre_keys = prefix_keys.reshape(-1, kv_heads, HD)]
    ppermute x1 -> x4, waiting for transfers between devices: 4.39 us -> 8.69 us  [shifted(): return lax.ppermute(value, axis, pairs)]
  transfers between devices with their start and end apart: 4 -> 4, of which waited for: 3 -> 2; matrix products, arithmetic and copies ran while one was open for 23% -> 0% of each run, Pallas kernels for 0% -> 30%
where the time goes in v2:
time: 36.1 us; the launch traced here: 35.9 us
  Pallas kernels  17.4 us (48%)
  starting transfers between devices  9.69 us (27%)
  waiting for transfers between devices  8.69 us (24%)
    pallas_call x3, Pallas kernels, partial(): pl.pallas_call(functools.partial(send_kernel, share, (shift, later), grou...  12.3 us
    ppermute x4, starting transfers between devices, shifted(): return lax.ppermute(value, axis, pairs)  9.69 us
    ppermute x4, waiting for transfers between devices, shifted(): return lax.ppermute(value, axis, pairs)  8.69 us
    pallas_call x1, Pallas kernels, local(): pl.pallas_call(functools.partial(own_kernel, share, group), in_specs=[SME...  2.83 us
    pallas_call x1, Pallas kernels, local(): pl.pallas_call(functools.partial(mix_kernel, aligned), in_specs=[SMEM, SM...  1.63 us
  transfers between devices with their start and end apart: 4, of which 2 were waited for; matrix products, arithmetic and copies ran while one was open for 0% of the time, Pallas kernels for 30%

profile of v2, /device:TPU:0, one launch (start us, length us, event | category | flops | bytes accessed | tf_op | source)
XLA Modules:
  0.0 35.9 jit_solution(8803247483476395306)
XLA Ops:
  0.0 0.0 copy-start
  0.0 4.3 %partial.3 = (bf16[800,128]{1,0:T(8,128)(2,1)S(1)}, bf16[3,16,2048]{2,1,0:T(8,128)(2,1)S(1)}, bf16[1536,128]{1,0:T(8,128)(2,1)S(1)}, bf16[1536,128]{1,0:T(8,128)...) custom-call(s32[16]{0:T(128)} %lengths.7, bf16[3,16,8192]{2,1,0:T(8,128)(2,1)} %refs_0_.5, ...), custom_call_target="tpu_custom_call" | custom-call | flops 603979776 | bytes 1310720 | tf_op jit(solution)/shard_map/partial/pallas_call | solution.py:363
  4.4 4.1 %collective-permute-start = (bf16[800,128]{1,0:T(8,128)(2,1)S(1)}, bf16[800,128]{1,0:T(8,128)(2,1)S(1)}, u32[]{:S(2)}, u32[]{:S(2)}) collective-permute-start(bf16[800,128]{1,0:T(8,128)(2,1)S(1)} %get-tuple-element.25), channel_id=1, source_target_pairs={{0,16},{8,24},{16,0},{24,8},{1,17},{9,25},{17,1},{25,9},{2,18},{10... | collective-permute-start | bytes 614408 | tf_op jit(solution)/shard_map/ppermute | solution.py:305
  8.5 0.0 copy-done
  8.5 4.0 %partial.4 = (bf16[800,128]{1,0:T(8,128)(2,1)S(1)}, bf16[3,16,2048]{2,1,0:T(8,128)(2,1)S(1)}, bf16[1536,128]{1,0:T(8,128)(2,1)S(1)}, bf16[1536,128]{1,0:T(8,128)...) custom-call(s32[16]{0:T(128)S(1)} %copy-done, bf16[3,16,8192]{2,1,0:T(8,128)(2,1)} %refs_0_.5, ...), custom_call_target="tpu_custom_call" | custom-call | flops 603979776 | bytes 1310720 | tf_op jit(solution)/shard_map/partial/pallas_call | solution.py:363
  12.5 1.6 %collective-permute-start.1 = (bf16[800,128]{1,0:T(8,128)(2,1)S(1)}, bf16[800,128]{1,0:T(8,128)(2,1)S(1)}, u32[]{:S(2)}, u32[]{:S(2)}) collective-permute-start(bf16[800,128]{1,0:T(8,128)(2,1)S(1)} %get-tuple-element.31), channel_id=1, source_target_pairs={{0,8},{8,16},{16,24},{24,0},{1,9},{9,17},{17,25},{25,1},{2,10},{10... | collective-permute-start | bytes 614408 | tf_op jit(solution)/shard_map/ppermute | solution.py:305
  14.2 0.0 copy-start.3
  14.2 0.0 copy-start.4
  14.2 4.0 %partial.5 = (bf16[800,128]{1,0:T(8,128)(2,1)S(1)}, bf16[3,16,2048]{2,1,0:T(8,128)(2,1)S(1)}, bf16[1536,128]{1,0:T(8,128)(2,1)S(1)}, bf16[1536,128]{1,0:T(8,128)...) custom-call(s32[16]{0:T(128)S(1)} %copy-done, bf16[3,16,8192]{2,1,0:T(8,128)(2,1)} %refs_0_.5, ...), custom_call_target="tpu_custom_call" | custom-call | flops 603979776 | bytes 1310720 | tf_op jit(solution)/shard_map/partial/pallas_call | solution.py:363
  18.1 2.3 %collective-permute-start.2 = (bf16[800,128]{1,0:T(8,128)(2,1)S(1)}, bf16[800,128]{1,0:T(8,128)(2,1)S(1)}, u32[]{:S(2)}, u32[]{:S(2)}) collective-permute-start(bf16[800,128]{1,0:T(8,128)(2,1)S(1)} %get-tuple-element.37), channel_id=1, source_target_pairs={{0,24},{8,0},{16,8},{24,16},{1,25},{9,1},{17,9},{25,17},{2,26},{10... | collective-permute-start | bytes 614408 | tf_op jit(solution)/shard_map/ppermute | solution.py:305
  20.4 0.0 copy-done.3
  20.4 0.0 copy-done.4
  20.4 0.0 copy-start.1
  20.4 0.0 copy-start.2
  20.4 2.8 %own.1 = (f32[768,128]{1,0:T(8,128)S(1)}, f32[8,128]{1,0:T(8,128)S(1)}) custom-call(s32[16]{0:T(128)S(1)} %copy-done, bf16[3,16,2048]{2,1,0:T(8,128)(2,1)S(1)} %get-tuple-element.38.refs_0_, bf16[1536,128]{1,0:T(8,128)(2,1)S(1)} %get-tuple-element.39.refs_1_, bf16[1536,128]{1,0:T(8,128)(2,1)S(1)} %get-tuple-element.40.refs_2_, ...), custom_call_target="tpu_custom_call" | custom-call | flops 603979776 | bytes 1310720 | tf_op jit(solution)/shard_map/own/pallas_call | solution.py:381
  23.2 0.0 collective-permute-done.refs_0_
  23.3 0.0 collective-permute-done.1.refs_1_
  23.3 3.5 %collective-permute-done.2.refs_2_ = bf16[800,128]{1,0:T(8,128)(2,1)S(1)} collective-permute-done((bf16[800,128]{1,0:T(8,128)(2,1)S(1)}, bf16[800,128]{1,0:T(8,128)(2,1)S(1)}, u32[]{:S(2)}, u32[]{:S(2)}) %collective-permute-start.2) | collective-permute-done | bytes 204832 | tf_op jit(solution)/shard_map/ppermute | solution.py:305
  26.7 0.7 %combine.1.a_ref = bf16[768,128]{1,0:T(8,128)(2,1)S(1)} custom-call(bf16[800,128]{1,0:T(8,128)(2,1)S(1)} %collective-permute-done.refs_0_, bf16[800,128]{1,0:T(8,128)(2,1)S(1)} %collective-permute-done.1.refs_1_, bf16[800,128]{1,0:T(8,128)(2,1)S(1)} %collective-permute-done.2.refs_2_, f32[768,128]{1,0:T(8,128)S(1)} %get-tuple-element.43.refs_3_, ...), custom_call_target="tpu_custom_call" | custom-call | tf_op jit(solution)/shard_map/combine/pallas_call | solution.py:394
  27.4 1.6 %collective-permute-start.3 = (bf16[768,128]{1,0:T(8,128)(2,1)S(1)}, bf16[768,128]{1,0:T(8,128)(2,1)S(1)}, u32[]{:S(2)}, u32[]{:S(2)}) collective-permute-start(bf16[768,128]{1,0:T(8,128)(2,1)S(1)} %combine.1.a_ref), channel_id=1, source_target_pairs={{0,4},{1,5},{2,6},{3,7},{4,0},{5,1},{6,2},{7,3},{8,12},{9,13},{10,... | collective-permute-start | bytes 589832 | tf_op jit(solution)/shard_map/ppermute | solution.py:305
  29.0 5.2 %collective-permute-done.3.b_ref = bf16[768,128]{1,0:T(8,128)(2,1)S(1)} collective-permute-done((bf16[768,128]{1,0:T(8,128)(2,1)S(1)}, bf16[768,128]{1,0:T(8,128)(2,1)S(1)}, u32[]{:S(2)}, u32[]{:S(2)}) %collective-permute-start.3) | collective-permute-done | bytes 196640 | tf_op jit(solution)/shard_map/ppermute | solution.py:305
  34.3 0.0 copy-done.1
  34.3 0.0 copy-done.2
  34.3 1.6 %mix.1 = bf16[3,16,2048]{2,1,0:T(8,128)(2,1)} custom-call(s32[128]{0:T(128)S(1)} %copy-done.1, f32[64]{0:T(128)S(1)} %copy-done.2, bf16[768,128]{1,0:T(8,128)(2,1)S(1)} %combine.1.a_ref, bf16[768,128]{1,0:T(8,128)(2,1)S(1)} %collective-permute-done.3.b_ref), custom_call_target="tpu_custom_call" | custom-call | tf_op jit(solution)/shard_map/mix/pallas_call | solution.py:409
Async XLA Ops:
  0.0 8.5 %copy-start = (s32[16]{0:T(128)S(1)}, s32[16]{0:T(128)}, u32[]{:S(2)}) copy-start(s32[16]{0:T(128)} %lengths.7) | copy-start | bytes 196
  4.4 18.9 %collective-permute-start = (bf16[800,128]{1,0:T(8,128)(2,1)S(1)}, bf16[800,128]{1,0:T(8,128)(2,1)S(1)}, u32[]{:S(2)}, u32[]{:S(2)}) collective-permute-start(bf16[800,128]{1,0:T(8,128)(2,1)S(1)} %get-tuple-element.25), channel_id=1, source_target_pairs={{0,16},{8,24},{16,0},{24,8},{1,17},{9,25},{17,1},{25,9},{2,18},{10... | collective-permute-start | bytes 614408 | tf_op jit(solution)/shard_map/ppermute | solution.py:305
  12.5 10.8 %collective-permute-start.1 = (bf16[800,128]{1,0:T(8,128)(2,1)S(1)}, bf16[800,128]{1,0:T(8,128)(2,1)S(1)}, u32[]{:S(2)}, u32[]{:S(2)}) collective-permute-start(bf16[800,128]{1,0:T(8,128)(2,1)S(1)} %get-tuple-element.31), channel_id=1, source_target_pairs={{0,8},{8,16},{16,24},{24,0},{1,9},{9,17},{17,25},{25,1},{2,10},{10... | collective-permute-start | bytes 614408 | tf_op jit(solution)/shard_map/ppermute | solution.py:305
  14.2 6.3 %copy-start.3 = (bf16[3,16,512]{2,1,0:T(8,128)(2,1)S(1)}, bf16[3,16,512]{2,1,0:T(8,128)(2,1)}, u32[]{:S(2)}) copy-start(bf16[3,16,512]{2,1,0:T(8,128)(2,1)} %refs_5_.1) | copy-start | bytes 147460
  14.2 6.3 %copy-start.4 = (bf16[3,16,512]{2,1,0:T(8,128)(2,1)S(1)}, bf16[3,16,512]{2,1,0:T(8,128)(2,1)}, u32[]{:S(2)}) copy-start(bf16[3,16,512]{2,1,0:T(8,128)(2,1)} %refs_6_.1) | copy-start | bytes 147460
  18.1 8.6 %collective-permute-start.2 = (bf16[800,128]{1,0:T(8,128)(2,1)S(1)}, bf16[800,128]{1,0:T(8,128)(2,1)S(1)}, u32[]{:S(2)}, u32[]{:S(2)}) collective-permute-start(bf16[800,128]{1,0:T(8,128)(2,1)S(1)} %get-tuple-element.37), channel_id=1, source_target_pairs={{0,24},{8,0},{16,8},{24,16},{1,25},{9,1},{17,9},{25,17},{2,26},{10... | collective-permute-start | bytes 614408 | tf_op jit(solution)/shard_map/ppermute | solution.py:305
  20.4 13.9 %copy-start.1 = (s32[128]{0:T(128)S(1)}, s32[128]{0:T(128)}, u32[]{:S(2)}) copy-start(s32[128]{0:T(128)} %pair_of.1) | copy-start | bytes 1540
  20.4 13.9 %copy-start.2 = (f32[64]{0:T(128)S(1)}, f32[64]{0:T(128)}, u32[]{:S(2)}) copy-start(f32[64]{0:T(128)} %guidance.1) | copy-start | bytes 772
  27.4 6.9 %collective-permute-start.3 = (bf16[768,128]{1,0:T(8,128)(2,1)S(1)}, bf16[768,128]{1,0:T(8,128)(2,1)S(1)}, u32[]{:S(2)}, u32[]{:S(2)}) collective-permute-start(bf16[768,128]{1,0:T(8,128)(2,1)S(1)} %combine.1.a_ref), channel_id=1, source_target_pairs={{0,4},{1,5},{2,6},{3,7},{4,0},{5,1},{6,2},{7,3},{8,12},{9,13},{10,... | collective-permute-start | bytes 589832 | tf_op jit(solution)/shard_map/ppermute | solution.py:305
